TPU v7x, 512 devices: a whole 4x8x8 slice. The times are simulated.
512 devices in a mesh: tile: 128 (over z_lo, y, x, core), layer: 4 (over z_hi).
Axes of the slice: x: 4, y: 8, z: 8 (z_hi: 4, z_lo: 2; z = z_hi * 2 + z_lo), core: 2. Of those that a mesh axis runs over, the one named last changes fastest.
Arguments:
- rand_vectors: bfloat16 [4, 16, 1572864], P(None, None, ('tile', 'layer')), may hold values from -4 to 4
- onsite: bfloat16 [12288, 128, 128], P(('tile', 'layer')), as said below
- down_hop: bfloat16 [12288, 128, 128], P(('tile', 'layer')), may hold values from -0.1875 to 0.1875
- right_hop: bfloat16 [12288, 128, 128], P(('tile', 'layer')), may hold values from -0.1875 to 0.1875
- pattern: int32 [12288, 2], P(('tile', 'layer')), may hold values 0 or 1
- pairing: float32 [1572864], P(('tile', 'layer')), may hold values from 0.1 to 1
- link_rows: int32 [65536, 8], P(('tile', 'layer')), may hold values from 0 to 3071
- link_target: int32 [65536, 8], P(('tile', 'layer')), may hold values from 0 to 3071
- link_weight: bfloat16 [65536, 8], P(('tile', 'layer')), may hold values from -3 to 3
- link_count: int32 [65536], P(('tile', 'layer')), may hold values from 0 to 8, as said below
Outputs:
- cheb_one: float32 [4, 16, 1572864], P(None, None, ('tile', 'layer'))
- cheb_two: float32 [4, 16, 1572864], P(None, None, ('tile', 'layer'))
- moments: float32 [3, 4, 1572864], P(None, None, ('tile', 'layer'))
Inputs may be any that keep to these rules, and one draw needn't show every extreme that they name: `onsite`: every tile is symmetric. `link_rows`: a local site of the sending device. `link_target`: a local site of the receiving device. `link_count`: the number of used slots from one source tile row index to one receiving device; loads differ strongly between receiving tile row indices.
All inputs are finite; a program needn't handle non-finite values. No bound on the sum of `pattern` on one device may be relied on, other than what follows from the above.
Results may differ from a plain program's by a relative error of at most 0.0025.
Values may be sent and summed in bfloat16 or wider, within the bound.
No kernel may reach another device: no remote copies, remote signals or barrier semaphores. Data moves between devices by JAX's collectives and lax.ppermute only.
A program may use at most 64 MiB of HBM per device.

v0:
```python
import jax
import jax.numpy as jnp
from jax import lax
from jax.sharding import PartitionSpec as P

TILE = 128
TR = 4
TC = 6


def passed_along(value, axis, by):
    length = lax.axis_size(axis)
    pairs = [(i, i + by) for i in range(length) if 0 <= i + by < length]
    return lax.ppermute(value, axis, pairs)


def partner_2(value, axis, bit):
    return lax.ppermute(value, axis, [(i, i ^ 1 << bit) for i in range(lax.axis_size(axis))])


def with_halo(block, sides, width):
    for axis, dim in sides:
        count = lax.axis_size(axis)
        forward = [(i, i + 1) for i in range(count - 1)]
        backward = [(target, source) for source, target in forward]
        low = lax.ppermute(
            lax.slice_in_dim(block, block.shape[dim] - width, None, axis=dim), axis, forward
        )
        high = lax.ppermute(lax.slice_in_dim(block, 0, width, axis=dim), axis, backward)
        block = jnp.concatenate([low, block, high], axis=dim)
    return block


def hop_forward(tiles, field_grid):
    return jnp.einsum("rkij,nrkj->nrki", tiles, field_grid, preferred_element_type=jnp.float32)


def hop_transposed(tiles, field_grid):
    return jnp.einsum("rkji,nrkj->nrki", tiles, field_grid, preferred_element_type=jnp.float32)


def shards(
    rand_vectors,
    onsite,
    down_hop,
    right_hop,
    pattern,
    pairing,
    link_rows,
    link_target,
    link_weight,
    link_count,
):
    components, vectors, sites_dev = rand_vectors.shape
    field_rows = components * vectors
    tile_count = lax.axis_size("tile")
    slot_count = link_rows.shape[1]
    self_tiles = onsite.reshape(TR, TC, TILE, TILE)
    down_mask = (down_hop * pattern[:, 0][:, None, None].astype(jnp.bfloat16)).reshape(
        TR, TC, TILE, TILE
    )
    right_mask = (right_hop * pattern[:, 1][:, None, None].astype(jnp.bfloat16)).reshape(
        TR, TC, TILE, TILE
    )
    is_left = lax.axis_index("layer") % 2 == 0
    slot_live = jnp.arange(slot_count, dtype=jnp.int32)[None, :] < link_count[:, None]
    slot_weight = jnp.where(slot_live, link_weight.astype(jnp.float32), 0.0).reshape(-1)
    send_rows = link_rows.reshape(-1)
    recv_sites = link_target.reshape(-1)
    upper_blocks = passed_along(down_mask[TR - 1], "tile", 1)
    shifted_down = jnp.concatenate([upper_blocks[None], down_mask[:-1]], axis=0)
    weight_table = slot_weight.reshape(tile_count, slot_count).astype(jnp.bfloat16)
    weight_spread = lax.all_to_all(weight_table, "tile", split_axis=0, concat_axis=0, tiled=True)
    sender_weight = partner_2(weight_spread, "layer", 1).astype(jnp.float32).reshape(-1)

    def apply_hop(field_b):
        field_grid = field_b.reshape(field_rows, TR, TC, TILE)
        accumulated = hop_forward(self_tiles, field_grid)
        padded = with_halo(field_grid, (("tile", 1),), 1)
        accumulated = (
            accumulated
            + hop_forward(down_mask, padded[:, 2:])
            + hop_transposed(shifted_down, padded[:, :-2])
        )
        leftward = hop_transposed(right_mask, field_grid)
        payload = jnp.where(
            is_left, leftward[:, :, TC - 1], field_grid[:, :, 0].astype(jnp.float32)
        )
        partner = partner_2(payload, "layer", 0)
        right_edge = jnp.where(is_left, partner, 0.0).astype(jnp.bfloat16)
        accumulated = accumulated + hop_forward(
            right_mask, jnp.concatenate([field_grid[:, :, 1:], right_edge[:, :, None]], axis=2)
        )
        left_edge = jnp.where(is_left, 0.0, partner)
        accumulated = accumulated + jnp.concatenate(
            [left_edge[:, :, None], leftward[:, :, :-1]], axis=2
        )
        accumulated = accumulated.reshape(field_rows, sites_dev)
        flat_field = field_b.reshape(field_rows, sites_dev)
        outgoing = jnp.take(flat_field, send_rows, axis=1).reshape(
            field_rows, tile_count, slot_count
        )
        own_ends = jnp.take(flat_field, recv_sites, axis=1).reshape(
            field_rows, tile_count, slot_count
        )
        paired = jnp.concatenate([outgoing, own_ends], axis=2)
        paired_spread = lax.all_to_all(paired, "tile", split_axis=1, concat_axis=1, tiled=True)
        landed = partner_2(paired_spread, "layer", 1)
        arrived_terms = (
            landed[:, :, :slot_count].reshape(field_rows, -1).astype(jnp.float32)
            * slot_weight[None, :]
        )
        accumulated = accumulated.at[:, recv_sites].add(arrived_terms)
        returned_terms = (
            landed[:, :, slot_count:].reshape(field_rows, -1).astype(jnp.float32)
            * sender_weight[None, :]
        )
        accumulated = accumulated.at[:, send_rows].add(returned_terms)
        return accumulated.reshape(components, vectors, sites_dev)

    nambu_sign = jnp.array([1.0, 1.0, -1.0, -1.0], dtype=jnp.float32)[:, None, None]
    initial = rand_vectors.astype(jnp.float32)
    cheb_one = nambu_sign * apply_hop(rand_vectors) + pairing * jnp.roll(initial, 2, axis=0)
    one_rounded = cheb_one.astype(jnp.bfloat16)
    cheb_two = (
        2.0 * (nambu_sign * apply_hop(one_rounded) + pairing * jnp.roll(cheb_one, 2, axis=0))
        - initial
    )
    moments = jnp.stack(
        [
            jnp.mean(initial * initial, axis=1),
            jnp.mean(initial * cheb_one, axis=1),
            jnp.mean(initial * cheb_two, axis=1),
        ]
    )
    return (cheb_one, cheb_two, moments)


def solution(mesh):
    in_specs = (
        P(None, None, ("tile", "layer")),
        P(("tile", "layer"), None, None),
        P(("tile", "layer"), None, None),
        P(("tile", "layer"), None, None),
        P(("tile", "layer"), None),
        P(("tile", "layer")),
        P(("tile", "layer"), None),
        P(("tile", "layer"), None),
        P(("tile", "layer"), None),
        P(("tile", "layer")),
    )
    out_specs = (
        P(None, None, ("tile", "layer")),
        P(None, None, ("tile", "layer")),
        P(None, None, ("tile", "layer")),
    )
    return jax.shard_map(shards, mesh=mesh, in_specs=in_specs, out_specs=out_specs, check_vma=False)
```

profile of v0, /device:TPU:7, one launch (start us, length us, event | category | flops | bytes accessed | tf_op | source)
XLA Modules:
  0.0 250.8 jit_solution(17171188428479891034)
XLA Ops:
  0.7 1.6 reshape.197
  3.7 5.8 %collective-permute-start.3 = (f32[64,4,128]{2,0,1:T(8,128)}, f32[64,4,128]{2,0,1:T(8,128)}, u32[]{:S(2)}, u32[]{:S(2)}) collective-permute-start(f32[64,4,128]{2,0,1:T(8,128)} %fusion.54), channel_id=1, source_target_pairs={{0,1},{1,0},{2,3},{3,2},{4,5},{5,4},{6,7},{7,6},{8,9},{9,8},{10,11... | collective-permute-start | bytes 393224 | tf_op jit(solution)/shard_map/ppermute | solution.py:18
  9.5 0.7 fusion.69
  10.2 2.9 %collective-permute-start = (bf16[64,1,6,128]{3,0,2,1:T(8,128)(2,1)}, bf16[64,1,6,128]{3,0,2,1:T(8,128)(2,1)}, u32[]{:S(2)}, u32[]{:S(2)}) collective-permute-start(bf16[64,1,6,128]{3,0,2,1:T(8,128)(2,1)} %get-tuple-element.17), channel_id=1, source_target_pairs={{4,0},{8,4},{12,8},{16,12},{20,16},{24,20},{28,24},{32,28},{36,32}... | collective-permute-start | bytes 294920 | tf_op jit(solution)/shard_map/ppermute | solution.py:29
  13.1 4.8 %collective-permute-start.1 = (bf16[64,1,6,128]{3,0,2,1:T(8,128)(2,1)}, bf16[64,1,6,128]{3,0,2,1:T(8,128)(2,1)}, u32[]{:S(2)}, u32[]{:S(2)}) collective-permute-start(bf16[64,1,6,128]{3,0,2,1:T(8,128)(2,1)} %get-tuple-element.16), channel_id=1, source_target_pairs={{0,4},{4,8},{8,12},{12,16},{16,20},{20,24},{24,28},{28,32},{32,36}... | collective-permute-start | bytes 294920 | tf_op jit(solution)/shard_map/ppermute | solution.py:26
  18.0 0.9 copy-done.2
  18.9 0.7 slice.135
  19.6 1.9 collective-permute-start.2
  21.6 0.7 copy.130
  22.3 13.1 %all-to-all-start.1 = ((bf16[128,1,8]{2,1,0:T(2,128)(2,1)}), bf16[128,1,8]{2,1,0:T(2,128)(2,1)S(1)}, u32[]{:S(2)}, u32[]{:S(2)}) async-start(bf16[128,1,8]{2,1,0:T(2,128)(2,1)} %copy.130), calls=%async_computation.1 | async-start | bytes 131072 | tf_op jit(solution)/shard_map/all_to_all | solution.py:73
  37.1 0.9 fusion.68
  38.0 1.5 fusion.72
  39.9 3.2 %gather_fusion = bf16[1024,64]{1,0:T(8,128)(2,1)S(1)} fusion(bf16[64,3072]{0,1:T(8,128)(2,1)S(1)} %copy.124, s32[1024]{0:T(1024)S(1)} %fusion.57), kind=kCustom, calls=%fused_computation.clone | custom fusion | bytes 266240 | tf_op jit(solution)/shard_map/jit(_take)/gather | solution.py:100
  43.2 4.3 %gather_fusion.1 = bf16[1024,64]{1,0:T(8,128)(2,1)} fusion(bf16[64,3072]{0,1:T(8,128)(2,1)S(1)} %copy.124, s32[1024]{0:T(1024)S(1)} %fusion.58), kind=kCustom, calls=%fused_computation.1.clone | custom fusion | bytes 266240 | tf_op jit(solution)/shard_map/jit(_take)/gather | solution.py:103
  48.1 1.3 select_bitcast_fusion.2
  49.4 0.9 fusion.71
  50.4 2.1 reshape.304
  52.5 12.9 %all-to-all-start = ((bf16[128,2,512]{2,1,0:T(2,128)(2,1)}), bf16[128,2,512]{2,1,0:T(2,128)(2,1)}, u32[]{:S(2)}, u32[]{:S(2)}) async-start(bf16[128,2,512]{2,1,0:T(2,128)(2,1)} %reshape.304), calls=%async_computation | async-start | bytes 524288 | tf_op jit(solution)/shard_map/all_to_all | solution.py:107
  66.1 7.9 %collective-permute-start.5 = (bf16[128,8]{0,1:T(8,128)(2,1)}, bf16[128,8]{0,1:T(8,128)(2,1)}, u32[]{:S(2)}, u32[]{:S(2)}) collective-permute-start(bf16[128,8]{0,1:T(8,128)(2,1)} %bitcast.27), channel_id=1, source_target_pairs={{0,2},{1,3},{2,0},{3,1},{4,6},{5,7},{6,4},{7,5},{8,10},{9,11},{10,... | collective-permute-start | bytes 6152 | tf_op jit(solution)/shard_map/ppermute | solution.py:18
  74.6 0.9 slice.136
  75.7 0.7 mul.135
  77.7 0.8 copy.132
  79.1 2.7 %convolution_add_fusion.3 = f32[4,6,64,128]{3,2,1,0:T(8,128)} fusion(f32[4,6,64,128]{3,2,1,0:T(8,128)} %fusion.72, bf16[4,6,128,128]{3,2,1,0:T(8,128)(2,1)S(1)} %bitcast.133, bf16[64,1,6,128]{3,0,2,1:T(8,128)(2,1)} %collective-permute-done, bf16[64,4,6,128]{3,0,2,1:T(8,128)(2,1)S(1)} %copy.110), kind=kOutput, calls=%fused_computation.20 | convolution fusion | flops 51511296 | bytes 2850816 | tf_op jit(solution)/shard_map/rkij,nrkj->nrki/dot_general | solution.py:35
  81.8 1.0 fusion.55
  82.8 1.5 fusion.42
  84.4 2.2 reshape.305
  86.5 5.1 %collective-permute-start.4 = (bf16[64,128,16]{0,2,1:T(8,128)(2,1)}, bf16[64,128,16]{0,2,1:T(8,128)(2,1)}, u32[]{:S(2)}, u32[]{:S(2)}) collective-permute-start(bf16[64,128,16]{0,2,1:T(8,128)(2,1)} %bitcast.110), channel_id=1, source_target_pairs={{0,2},{1,3},{2,0},{3,1},{4,6},{5,7},{6,4},{7,5},{8,10},{9,11},{10,... | collective-permute-start | bytes 786440 | tf_op jit(solution)/shard_map/ppermute | solution.py:18
  91.7 2.9 %fusion.5 = f32[64,4,6,128]{3,0,2,1:T(8,128)} fusion(f32[4,6,64,128]{3,2,1,0:T(8,128)} %fusion.42, f32[4,6,64,128]{3,2,1,0:T(8,128)} %convolution_add_fusion.3, f32[64,4,5,128]{3,0,2,1:T(8,128)S(1)} %slice-done, f32[64,4,1,128]{3,0,2,1:T(8,128)S(1)} %select_bitcast_fusion.5, bf16[64,4,6,128]{3,0,2,1:T(8,128)(2,1)S(1)} %copy.110, ...), kind=kOutput, calls=%fused_computation.19 | convolution fusion | flops 53673984 | bytes 4423680 | tf_op jit(solution)/shard_map/rkji,nrkj->nrki/dot_general | solution.py:39
  94.6 1.6 copy.166
  96.2 20.6 %collective-permute-done.4 = bf16[64,128,16]{0,2,1:T(8,128)(2,1)} collective-permute-done((bf16[64,128,16]{0,2,1:T(8,128)(2,1)}, bf16[64,128,16]{0,2,1:T(8,128)(2,1)}, u32[]{:S(2)}, u32[]{:S(2)}) %collective-permute-start.4) | collective-permute-done | bytes 262176 | tf_op jit(solution)/shard_map/ppermute | solution.py:18
  116.8 7.1 %scatter_custom_fusion = f32[64,3072]{0,1:T(8,128)S(1)} fusion(f32[64,3072]{0,1:T(8,128)S(1)} %bitcast.126, s32[1024]{0:T(1024)} %bitcast.140, bf16[64,128,16]{0,2,1:T(8,128)(2,1)} %collective-permute-done.4, f32[1024]{0:T(1024)S(1)} %mul.125), kind=kCustom, calls=%fused_computation.54 | custom fusion | flops 196608 | bytes 1052672 | tf_op jit(solution)/shard_map/scatter-add | solution.py:113
  123.9 7.5 %scatter_custom_fusion.1 = f32[64,3072]{0,1:T(8,128)S(1)} fusion(f32[64,3072]{0,1:T(8,128)S(1)} %scatter_custom_fusion, s32[1024]{0:T(1024)} %bitcast.142, bf16[64,128,16]{0,2,1:T(8,128)(2,1)} %collective-permute-done.4, f32[1024]{0:T(1024)} %reshape.217), kind=kCustom, calls=%fused_computation.51 | custom fusion | flops 196608 | bytes 1052672 | tf_op jit(solution)/shard_map/scatter-add | solution.py:118
  131.4 1.3 copy.133
  132.7 2.6 %pad_maximum_fusion.1 = (f32[4,16,3072]{2,1,0:T(8,128)}, f32[4,16,3072]{2,1,0:T(8,128)}) fusion(f32[2,16,3072]{2,1,0:T(8,128)} %get-tuple-element.15, f32[2,16,3072]{2,1,0:T(8,128)} %get-tuple-element.14, f32[3072]{0:T(1024)S(1)} %copy-done.13, f32[4,16,3072]{2,1,0:T(8,128)} %bitcast.137, f32[4]{0:T(128)} %constant.42.clone), kind=kLoop, calls=%fused_computation.22 | loop fusion | flops 786432 | bytes 3158032 | tf_op jit(solution)/shard_map/jit(_roll_static)/concatenate | solution.py:123
  135.3 2.8 %copy.149 = f32[64,3072]{0,1:T(8,128)} copy(f32[64,3072]{1,0:T(8,128)} %bitcast.135) | data formatting | bytes 1572864 | tf_op jit(solution)/shard_map/jit(_roll_static)/concatenate | solution.py:123
  138.1 2.8 %add_convert_fusion = bf16[64,3072]{0,1:T(8,128)(2,1)} fusion(f32[64,3072]{0,1:T(8,128)} %copy.149, f32[64,3072]{0,1:T(8,128)S(1)} %scatter_custom_fusion.1, f32[3072]{0:T(1024)S(1)} %copy-done.13, f32[64]{0:T(128)} %mul.136), kind=kLoop, calls=%fused_computation.8 | loop fusion | flops 786432 | bytes 1978624 | tf_op jit(solution)/shard_map/convert_element_type | solution.py:124
  140.9 5.6 %gather_fusion.2 = bf16[1024,64]{1,0:T(8,128)(2,1)} fusion(bf16[64,3072]{0,1:T(8,128)(2,1)} %add_convert_fusion, s32[1024]{0:T(1024)} %copy-done.16), kind=kCustom, calls=%fused_computation.2.clone | custom fusion | bytes 266240 | tf_op jit(solution)/shard_map/jit(_take)/gather | solution.py:100
  146.5 5.6 %gather_fusion.3 = bf16[1024,64]{1,0:T(8,128)(2,1)} fusion(bf16[64,3072]{0,1:T(8,128)(2,1)} %add_convert_fusion, s32[1024]{0:T(1024)} %copy-done.15), kind=kCustom, calls=%fused_computation.3.clone | custom fusion | bytes 266240 | tf_op jit(solution)/shard_map/jit(_take)/gather | solution.py:103
  152.1 2.5 %concatenate.53 = f32[64,4,6,128]{3,2,1,0:T(8,128)} reshape(f32[4,16,3072]{2,1,0:T(8,128)} %get-tuple-element.8) | data formatting | bytes 1572864 | tf_op jit(solution)/shard_map/jit(_roll_static)/concatenate | solution.py:123
  154.7 1.3 copy.135
  156.0 2.0 fusion.14
  158.0 0.7 fusion.67
  158.7 1.2 convolution_bitcast_fusion.1
  160.4 0.9 fusion.70
  161.3 2.1 reshape.306
  163.4 13.8 %all-to-all-start.2 = ((bf16[128,2,512]{2,1,0:T(2,128)(2,1)}), bf16[128,2,512]{2,1,0:T(2,128)(2,1)}, u32[]{:S(2)}, u32[]{:S(2)}) async-start(bf16[128,2,512]{2,1,0:T(2,128)(2,1)} %reshape.306), calls=%async_computation.2 | async-start | bytes 524288 | tf_op jit(solution)/shard_map/all_to_all | solution.py:107
  177.2 2.3 collective-permute-start.6
  179.5 0.9 fusion.53
  180.4 1.9 collective-permute-start.8
  182.4 5.6 %collective-permute-start.7 = (bf16[64,1,6,128]{3,0,1,2:T(8,128)(2,1)}, bf16[64,1,6,128]{3,0,1,2:T(8,128)(2,1)}, u32[]{:S(2)}, u32[]{:S(2)}) collective-permute-start(bf16[64,1,6,128]{3,0,1,2:T(8,128)(2,1)} %get-tuple-element.12), channel_id=1, source_target_pairs={{0,4},{4,8},{8,12},{12,16},{16,20},{20,24},{24,28},{28,32},{32,36}... | collective-permute-start | bytes 294920 | tf_op jit(solution)/shard_map/ppermute | solution.py:26
  188.0 0.8 fusion.66
  189.9 0.9 slice.150
  190.9 1.5 convolution_add_fusion.1
  192.4 1.5 fusion.15
  194.6 2.1 reshape.307
  196.7 4.8 %collective-permute-start.9 = (bf16[64,128,16]{0,2,1:T(8,128)(2,1)}, bf16[64,128,16]{0,2,1:T(8,128)(2,1)}, u32[]{:S(2)}, u32[]{:S(2)}) collective-permute-start(bf16[64,128,16]{0,2,1:T(8,128)(2,1)} %bitcast.112), channel_id=1, source_target_pairs={{0,2},{1,3},{2,0},{3,1},{4,6},{5,7},{6,4},{7,5},{8,10},{9,11},{10,... | collective-permute-start | bytes 786440 | tf_op jit(solution)/shard_map/ppermute | solution.py:18
  201.6 2.2 fusion.2
  203.8 1.7 copy.169
  205.5 22.5 %collective-permute-done.9 = bf16[64,128,16]{0,2,1:T(8,128)(2,1)} collective-permute-done((bf16[64,128,16]{0,2,1:T(8,128)(2,1)}, bf16[64,128,16]{0,2,1:T(8,128)(2,1)}, u32[]{:S(2)}, u32[]{:S(2)}) %collective-permute-start.9) | collective-permute-done | bytes 262176 | tf_op jit(solution)/shard_map/ppermute | solution.py:18
  228.0 9.4 %scatter_custom_fusion.2 = f32[64,3072]{0,1:T(8,128)} fusion(f32[64,3072]{0,1:T(8,128)} %bitcast.136, s32[1024]{0:T(1024)} %bitcast.141, bf16[64,128,16]{0,2,1:T(8,128)(2,1)} %collective-permute-done.9, f32[1024]{0:T(1024)S(1)} %mul.125), kind=kCustom, calls=%fused_computation.48 | custom fusion | flops 196608 | bytes 1052672 | tf_op jit(solution)/shard_map/scatter-add | solution.py:113
  237.4 9.4 %scatter_custom_fusion.3 = f32[64,3072]{0,1:T(8,128)} fusion(f32[64,3072]{0,1:T(8,128)} %scatter_custom_fusion.2, s32[1024]{0:T(1024)} %bitcast.143, bf16[64,128,16]{0,2,1:T(8,128)(2,1)} %collective-permute-done.9, f32[1024]{0:T(1024)S(1)} %copy-done.14), kind=kCustom, calls=%fused_computation.45 | custom fusion | flops 196608 | bytes 1052672 | tf_op jit(solution)/shard_map/scatter-add | solution.py:118
  246.9 1.9 copy.151
  248.8 1.2 multiply_reduce_fusion.2
  250.1 0.7 pad_maximum_fusion.4
  (101 shorter events, 9.9 us)
Async XLA Ops:
  0.6 37.4 %copy-start = (bf16[24,128,128]{2,1,0:T(8,128)(2,1)S(1)}, bf16[24,128,128]{2,1,0:T(8,128)(2,1)}, u32[]{:S(2)}) copy-start(bf16[24,128,128]{2,1,0:T(8,128)(2,1)} %param.14) | copy-start | bytes 2359300
  0.6 1.8 copy-start.24
  0.7 1.8 copy-start.9
  2.6 15.3 %copy-start.10 = (bf16[24,128,128]{2,1,0:T(8,128)(2,1)S(1)}, bf16[24,128,128]{2,1,0:T(8,128)(2,1)}, u32[]{:S(2)}) copy-start(bf16[24,128,128]{2,1,0:T(8,128)(2,1)} %param.15) | copy-start | bytes 2359300
  3.0 14.9 %copy-start.6 = (f32[64,4,6,128]{3,0,2,1:T(8,128)}, f32[64,4,6,128]{3,0,2,1:T(8,128)S(1)}, u32[]{:S(2)}) copy-start(f32[64,4,6,128]{3,0,2,1:T(8,128)S(1)} %convolution_bitcast_fusion) | copy-start | bytes 2359300
  3.0 18.6 %copy-start.22 = (bf16[128,8]{0,1:T(8,128)(2,1)S(1)}, bf16[128,8]{0,1:T(8,128)(2,1)}, u32[]{:S(2)}) copy-start(bf16[128,8]{0,1:T(8,128)(2,1)} %param.21) | copy-start | bytes 6148
  3.0 18.6 %copy-start.23 = (s32[128]{0:T(128)S(1)}, s32[128]{0:T(128)}, u32[]{:S(2)}) copy-start(s32[128]{0:T(128)} %param.22) | copy-start | bytes 1540
  3.0 32.4 %copy-start.20 = (s32[128,8]{0,1:T(8,128)S(1)}, s32[128,8]{0,1:T(8,128)}, u32[]{:S(2)}) copy-start(s32[128,8]{0,1:T(8,128)} %param.20) | copy-start | bytes 12292
  3.0 33.2 %copy-start.21 = (s32[128,8]{0,1:T(8,128)S(1)}, s32[128,8]{0,1:T(8,128)}, u32[]{:S(2)}) copy-start(s32[128,8]{0,1:T(8,128)} %param.19) | copy-start | bytes 12292
  3.0 34.1 %copy-start.1 = (bf16[4,16,3072]{2,1,0:T(8,128)(2,1)S(1)}, bf16[4,16,3072]{2,1,0:T(8,128)(2,1)}, u32[]{:S(2)}) copy-start(bf16[4,16,3072]{2,1,0:T(8,128)(2,1)} %param.13) | copy-start | bytes 1179652
  3.7 78.1 %collective-permute-start.3 = (f32[64,4,128]{2,0,1:T(8,128)}, f32[64,4,128]{2,0,1:T(8,128)}, u32[]{:S(2)}, u32[]{:S(2)}) collective-permute-start(f32[64,4,128]{2,0,1:T(8,128)} %fusion.54), channel_id=1, source_target_pairs={{0,1},{1,0},{2,3},{3,2},{4,5},{5,4},{6,7},{7,6},{8,9},{9,8},{10,11... | collective-permute-start | bytes 393224 | tf_op jit(solution)/shard_map/ppermute | solution.py:18
  10.2 68.9 %collective-permute-start = (bf16[64,1,6,128]{3,0,2,1:T(8,128)(2,1)}, bf16[64,1,6,128]{3,0,2,1:T(8,128)(2,1)}, u32[]{:S(2)}, u32[]{:S(2)}) collective-permute-start(bf16[64,1,6,128]{3,0,2,1:T(8,128)(2,1)} %get-tuple-element.17), channel_id=1, source_target_pairs={{4,0},{8,4},{12,8},{16,12},{20,16},{24,20},{28,24},{32,28},{36,32}... | collective-permute-start | bytes 294920 | tf_op jit(solution)/shard_map/ppermute | solution.py:29
  13.1 78.6 %collective-permute-start.1 = (bf16[64,1,6,128]{3,0,2,1:T(8,128)(2,1)}, bf16[64,1,6,128]{3,0,2,1:T(8,128)(2,1)}, u32[]{:S(2)}, u32[]{:S(2)}) collective-permute-start(bf16[64,1,6,128]{3,0,2,1:T(8,128)(2,1)} %get-tuple-element.16), channel_id=1, source_target_pairs={{0,4},{4,8},{8,12},{12,16},{16,20},{20,24},{24,28},{28,32},{32,36}... | collective-permute-start | bytes 294920 | tf_op jit(solution)/shard_map/ppermute | solution.py:26
  18.0 0.9 copy-start.2
  19.6 72.0 %collective-permute-start.2 = (bf16[6,128,128]{2,1,0:T(8,128)(2,1)}, bf16[6,128,128]{2,1,0:T(8,128)(2,1)}, u32[]{:S(2)}, u32[]{:S(2)}) collective-permute-start(bf16[6,128,128]{2,1,0:T(8,128)(2,1)} %slice.135), channel_id=1, source_target_pairs={{0,4},{4,8},{8,12},{12,16},{16,20},{20,24},{24,28},{28,32},{32,36}... | collective-permute-start | bytes 589832 | tf_op jit(solution)/shard_map/ppermute | solution.py:14
  22.3 30.2 %all-to-all-start.1 = ((bf16[128,1,8]{2,1,0:T(2,128)(2,1)}), bf16[128,1,8]{2,1,0:T(2,128)(2,1)S(1)}, u32[]{:S(2)}, u32[]{:S(2)}) async-start(bf16[128,1,8]{2,1,0:T(2,128)(2,1)} %copy.130), calls=%async_computation.1 | async-start | bytes 131072 | tf_op jit(solution)/shard_map/all_to_all | solution.py:73
  35.6 7.5 %copy-start.15 = (s32[1024]{0:T(1024)}, s32[1024]{0:T(1024)S(1)}, u32[]{:S(2)}) copy-start(s32[1024]{0:T(1024)S(1)} %fusion.58) | copy-start | bytes 12292
  36.4 3.5 %copy-start.16 = (s32[1024]{0:T(1024)}, s32[1024]{0:T(1024)S(1)}, u32[]{:S(2)}) copy-start(s32[1024]{0:T(1024)S(1)} %fusion.57) | copy-start | bytes 12292
  50.4 24.3 %copy-start.3 = (bf16[24,128,128]{2,1,0:T(8,128)(2,1)S(1)}, bf16[24,128,128]{2,1,0:T(8,128)(2,1)}, u32[]{:S(2)}) copy-start(bf16[24,128,128]{2,1,0:T(8,128)(2,1)} %copy-done.2) | copy-start | bytes 2359300
  52.5 31.8 %all-to-all-start = ((bf16[128,2,512]{2,1,0:T(2,128)(2,1)}), bf16[128,2,512]{2,1,0:T(2,128)(2,1)}, u32[]{:S(2)}, u32[]{:S(2)}) async-start(bf16[128,2,512]{2,1,0:T(2,128)(2,1)} %reshape.304), calls=%async_computation | async-start | bytes 524288 | tf_op jit(solution)/shard_map/all_to_all | solution.py:107
  66.1 11.6 %collective-permute-start.5 = (bf16[128,8]{0,1:T(8,128)(2,1)}, bf16[128,8]{0,1:T(8,128)(2,1)}, u32[]{:S(2)}, u32[]{:S(2)}) collective-permute-start(bf16[128,8]{0,1:T(8,128)(2,1)} %bitcast.27), channel_id=1, source_target_pairs={{0,2},{1,3},{2,0},{3,1},{4,6},{5,7},{6,4},{7,5},{8,10},{9,11},{10,... | collective-permute-start | bytes 6152 | tf_op jit(solution)/shard_map/ppermute | solution.py:18
  74.6 2.5 copy-start.13
  81.8 9.9 %slice-start = ((f32[64,4,6,128]{3,0,2,1:T(8,128)}), f32[64,4,5,128]{3,0,2,1:T(8,128)S(1)}, s32[]{:S(2)}) async-start(f32[64,4,6,128]{3,0,2,1:T(8,128)} %copy-done.6), calls=%async_computation.3 | async-start | bytes 1310720 | tf_op jit(solution)/shard_map/slice | solution.py:96
  86.5 30.3 %collective-permute-start.4 = (bf16[64,128,16]{0,2,1:T(8,128)(2,1)}, bf16[64,128,16]{0,2,1:T(8,128)(2,1)}, u32[]{:S(2)}, u32[]{:S(2)}) collective-permute-start(bf16[64,128,16]{0,2,1:T(8,128)(2,1)} %bitcast.110), channel_id=1, source_target_pairs={{0,2},{1,3},{2,0},{3,1},{4,6},{5,7},{6,4},{7,5},{8,10},{9,11},{10,... | collective-permute-start | bytes 786440 | tf_op jit(solution)/shard_map/ppermute | solution.py:18
  158.0 1.9 copy-start.12
  158.0 1.9 copy-start.18
  158.0 2.1 copy-start.11
  158.0 2.1 copy-start.17
  160.2 27.8 %copy-start.5 = (f32[4,16,3072]{2,1,0:T(8,128)S(1)}, f32[4,16,3072]{2,1,0:T(8,128)}, u32[]{:S(2)}) copy-start(f32[4,16,3072]{2,1,0:T(8,128)} %get-tuple-element.9) | copy-start | bytes 2359300
  163.4 31.2 %all-to-all-start.2 = ((bf16[128,2,512]{2,1,0:T(2,128)(2,1)}), bf16[128,2,512]{2,1,0:T(2,128)(2,1)}, u32[]{:S(2)}, u32[]{:S(2)}) async-start(bf16[128,2,512]{2,1,0:T(2,128)(2,1)} %reshape.306), calls=%async_computation.2 | async-start | bytes 524288 | tf_op jit(solution)/shard_map/all_to_all | solution.py:107
  177.2 13.6 %collective-permute-start.6 = (bf16[64,1,6,128]{3,0,1,2:T(8,128)(2,1)}, bf16[64,1,6,128]{3,0,1,2:T(8,128)(2,1)S(1)}, u32[]{:S(2)}, u32[]{:S(2)}) collective-permute-start(bf16[64,1,6,128]{3,0,1,2:T(8,128)(2,1)} %get-tuple-element.13), channel_id=1, source_target_pairs={{4,0},{8,4},{12,8},{16,12},{20,16},{24,20},{28,24},{32,28},{36,32}... | collective-permute-start | bytes 294920 | tf_op jit(solution)/shard_map/ppermute | solution.py:29
  180.4 11.9 %collective-permute-start.8 = (f32[64,4,128]{2,0,1:T(8,128)S(1)}, f32[64,4,128]{2,0,1:T(8,128)S(1)}, u32[]{:S(2)}, u32[]{:S(2)}) collective-permute-start(f32[64,4,128]{2,0,1:T(8,128)S(1)} %fusion.53), channel_id=1, source_target_pairs={{0,1},{1,0},{2,3},{3,2},{4,5},{5,4},{6,7},{7,6},{8,9},{9,8},{10,11... | collective-permute-start | bytes 393224 | tf_op jit(solution)/shard_map/ppermute | solution.py:18
  182.4 19.2 %collective-permute-start.7 = (bf16[64,1,6,128]{3,0,1,2:T(8,128)(2,1)}, bf16[64,1,6,128]{3,0,1,2:T(8,128)(2,1)}, u32[]{:S(2)}, u32[]{:S(2)}) collective-permute-start(bf16[64,1,6,128]{3,0,1,2:T(8,128)(2,1)} %get-tuple-element.12), channel_id=1, source_target_pairs={{0,4},{4,8},{8,12},{12,16},{16,20},{20,24},{24,28},{28,32},{32,36}... | collective-permute-start | bytes 294920 | tf_op jit(solution)/shard_map/ppermute | solution.py:26
  188.8 1.1 copy-start.7
  188.8 2.1 copy-start.4
  196.7 31.3 %collective-permute-start.9 = (bf16[64,128,16]{0,2,1:T(8,128)(2,1)}, bf16[64,128,16]{0,2,1:T(8,128)(2,1)}, u32[]{:S(2)}, u32[]{:S(2)}) collective-permute-start(bf16[64,128,16]{0,2,1:T(8,128)(2,1)} %bitcast.112), channel_id=1, source_target_pairs={{0,2},{1,3},{2,0},{3,1},{4,6},{5,7},{6,4},{7,5},{8,10},{9,11},{10,... | collective-permute-start | bytes 786440 | tf_op jit(solution)/shard_map/ppermute | solution.py:18
  203.8 33.6 %copy-start.14 = (f32[1024]{0:T(1024)S(1)}, f32[1024]{0:T(1024)}, u32[]{:S(2)}) copy-start(f32[1024]{0:T(1024)} %reshape.217) | copy-start | bytes 12292
  246.9 1.9 copy-start.8
  246.9 1.9 copy-start.19
where the time goes:
time: 252 us; the launch traced here: 251 us
  starting transfers between devices  82.9 us (33%)
  local copies, waits for them, and re-layouts  55.3 us (22%)
  other arithmetic  52.2 us (21%)
  waiting for transfers between devices  43.1 us (17%)
  matrix products  16 us (6%)
    ppermute x5, waiting for transfers between devices, partner_2(): lax.ppermute(value, axis, [(i, i ^ 1 << bit) for i in range(lax.axis_size...  43.1 us
    all_to_all x2, starting transfers between devices, apply_hop(): lax.all_to_all(paired, 'tile', split_axis=1, concat_axis=1, tiled=True)  26.7 us
    ppermute x5, starting transfers between devices, partner_2(): lax.ppermute(value, axis, [(i, i ^ 1 << bit) for i in range(lax.axis_size...  25.6 us
    scatter-add x2, other arithmetic, apply_hop(): accumulated = accumulated.at[:, send_rows].add(returned_terms)  16.9 us
    scatter-add x2, other arithmetic, apply_hop(): accumulated = accumulated.at[:, recv_sites].add(arrived_terms)  16.6 us
    all_to_all x1, starting transfers between devices, shards(): lax.all_to_all(weight_table, 'tile', split_axis=0, concat_axis=0, tiled=T...  13.1 us
    ppermute x2, starting transfers between devices, with_halo(): lax.ppermute(lax.slice_in_dim(block, block.shape[dim] - width, None, axis...  10.4 us
    unnamed x56, local copies, waits for them, and re-layouts  10.2 us
  transfers between devices with their start and end apart: 13, of which 2 were waited for; matrix products, arithmetic and copies ran while one was open for 20% of the time, Pallas kernels for 0%

commit v1 on v0

--- a/solution.py
+++ b/solution.py
@@ -104,7 +104,12 @@
             field_rows, tile_count, slot_count
         )
         paired = jnp.concatenate([outgoing, own_ends], axis=2)
-        paired_spread = lax.all_to_all(paired, "tile", split_axis=1, concat_axis=1, tiled=True)
+        paired_spread = jnp.concatenate(
+            lax.all_to_all(
+                jnp.stack(jnp.split(paired, lax.axis_size("tile"), axis=1)), "tile", 0, 0
+            ),
+            axis=1,
+        )
         landed = partner_2(paired_spread, "layer", 1)
         arrived_terms = (
             landed[:, :, :slot_count].reshape(field_rows, -1).astype(jnp.float32)

time: 252 us -> 259 us (1.028)
  local copies, waits for them, and re-layouts: 55.3 us -> 58.9 us
  waiting for transfers between devices: 43.1 us -> 40.2 us
    ppermute x5, waiting for transfers between devices: 43.1 us -> 40.2 us  [partner_2(): lax.ppermute(value, axis, [(i, i ^ 1 << bit) for i in range(lax.axis_size...]
    reshape x0 -> x2, local copies, waits for them, and re-layouts: none -> 2.73 us  [apply_hop(): jnp.concatenate(lax.all_to_all(jnp.stack(jnp.split(paired, lax.axis_size(...]
    unnamed x56 -> x62, local copies, waits for them, and re-layouts: 10.2 us -> 10.9 us
  transfers between devices with their start and end apart: 13 -> 13, of which waited for: 2 -> 2; matrix products, arithmetic and copies ran while one was open for 20% -> 21% of each run, Pallas kernels for 0% -> 0%
where the time goes in v1:
time: 259 us; the launch traced here: 256 us
  starting transfers between devices  83.1 us (32%)
  local copies, waits for them, and re-layouts  58.9 us (23%)
  other arithmetic  54.7 us (21%)
  waiting for transfers between devices  40.2 us (16%)
  matrix products  16.7 us (6%)
    ppermute x5, waiting for transfers between devices, partner_2(): lax.ppermute(value, axis, [(i, i ^ 1 << bit) for i in range(lax.axis_size...  40.2 us
    all_to_all x2, starting transfers between devices, apply_hop(): lax.all_to_all(jnp.stack(jnp.split(paired, lax.axis_size('tile'), axis=1)...  26.8 us
    ppermute x5, starting transfers between devices, partner_2(): lax.ppermute(value, axis, [(i, i ^ 1 << bit) for i in range(lax.axis_size...  25.7 us
    scatter-add x2, other arithmetic, apply_hop(): accumulated = accumulated.at[:, send_rows].add(returned_terms)  16.9 us
    scatter-add x2, other arithmetic, apply_hop(): accumulated = accumulated.at[:, recv_sites].add(arrived_terms)  16.5 us
    all_to_all x1, starting transfers between devices, shards(): lax.all_to_all(weight_table, 'tile', split_axis=0, concat_axis=0, tiled=T...  13.1 us
    unnamed x62, local copies, waits for them, and re-layouts  10.9 us
    ppermute x2, starting transfers between devices, with_halo(): lax.ppermute(lax.slice_in_dim(block, block.shape[dim] - width, None, axis...  10.4 us
  transfers between devices with their start and end apart: 13, of which 2 were waited for; matrix products, arithmetic and copies ran while one was open for 21% of the time, Pallas kernels for 0%

profile of v1, /device:TPU:7, one launch (start us, length us, event | category | flops | bytes accessed | tf_op | source)
XLA Modules:
  0.0 255.7 jit_solution(4230194438224088174)
XLA Ops:
  0.7 1.6 reshape.209
  3.7 5.8 %collective-permute-start.3 = (f32[64,4,128]{2,0,1:T(8,128)}, f32[64,4,128]{2,0,1:T(8,128)}, u32[]{:S(2)}, u32[]{:S(2)}) collective-permute-start(f32[64,4,128]{2,0,1:T(8,128)} %fusion.54), channel_id=1, source_target_pairs={{0,1},{1,0},{2,3},{3,2},{4,5},{5,4},{6,7},{7,6},{8,9},{9,8},{10,11... | collective-permute-start | bytes 393224 | tf_op jit(solution)/shard_map/ppermute | solution.py:18
  10.2 2.9 %collective-permute-start = (bf16[64,1,6,128]{3,0,2,1:T(8,128)(2,1)}, bf16[64,1,6,128]{3,0,2,1:T(8,128)(2,1)}, u32[]{:S(2)}, u32[]{:S(2)}) collective-permute-start(bf16[64,1,6,128]{3,0,2,1:T(8,128)(2,1)} %get-tuple-element.17), channel_id=1, source_target_pairs={{4,0},{8,4},{12,8},{16,12},{20,16},{24,20},{28,24},{32,28},{36,32}... | collective-permute-start | bytes 294920 | tf_op jit(solution)/shard_map/ppermute | solution.py:29
  13.1 4.8 %collective-permute-start.1 = (bf16[64,1,6,128]{3,0,2,1:T(8,128)(2,1)}, bf16[64,1,6,128]{3,0,2,1:T(8,128)(2,1)}, u32[]{:S(2)}, u32[]{:S(2)}) collective-permute-start(bf16[64,1,6,128]{3,0,2,1:T(8,128)(2,1)} %get-tuple-element.16), channel_id=1, source_target_pairs={{0,4},{4,8},{8,12},{12,16},{16,20},{20,24},{24,28},{28,32},{32,36}... | collective-permute-start | bytes 294920 | tf_op jit(solution)/shard_map/ppermute | solution.py:26
  18.0 0.9 copy-done.2
  18.9 0.7 slice.135
  19.6 1.9 collective-permute-start.2
  21.6 0.8 copy.130
  22.3 13.1 %all-to-all-start.1 = ((bf16[128,1,8]{2,1,0:T(2,128)(2,1)}), bf16[128,1,8]{2,1,0:T(2,128)(2,1)S(1)}, u32[]{:S(2)}, u32[]{:S(2)}) async-start(bf16[128,1,8]{2,1,0:T(2,128)(2,1)} %copy.130), calls=%async_computation.1 | async-start | bytes 131072 | tf_op jit(solution)/shard_map/all_to_all | solution.py:73
  37.1 0.9 fusion.324
  38.4 3.2 %gather_fusion.1 = bf16[1024,64]{1,0:T(8,128)(2,1)S(1)} fusion(bf16[64,3072]{0,1:T(8,128)(2,1)S(1)} %copy.124, s32[1024]{0:T(1024)S(1)} %get-tuple-element.23), kind=kCustom, calls=%fused_computation.1.clone | custom fusion | bytes 266240 | tf_op jit(solution)/shard_map/jit(_take)/gather | solution.py:103
  41.7 4.3 %gather_fusion = bf16[1024,64]{1,0:T(8,128)(2,1)} fusion(bf16[64,3072]{0,1:T(8,128)(2,1)S(1)} %copy.124, s32[1024]{0:T(1024)S(1)} %get-tuple-element.22), kind=kCustom, calls=%fused_computation.clone | custom fusion | bytes 266240 | tf_op jit(solution)/shard_map/jit(_take)/gather | solution.py:100
  46.0 0.9 select_bitcast_fusion.2
  46.8 1.2 select_bitcast_fusion.3
  49.9 1.5 fusion.326
  52.1 0.7 copy-done.12
  52.8 2.1 reshape.320
  55.0 12.9 %all-to-all-start = ((bf16[128,2,512]{2,1,0:T(2,128)(2,1)}), bf16[128,2,512]{2,1,0:T(2,128)(2,1)}, u32[]{:S(2)}, u32[]{:S(2)}) async-start(bf16[128,2,512]{2,1,0:T(2,128)(2,1)} %reshape.320), calls=%async_computation | async-start | bytes 524288 | tf_op jit(solution)/shard_map/all_to_all | solution.py:108
  68.5 7.9 %collective-permute-start.5 = (bf16[128,8]{0,1:T(8,128)(2,1)}, bf16[128,8]{0,1:T(8,128)(2,1)}, u32[]{:S(2)}, u32[]{:S(2)}) collective-permute-start(bf16[128,8]{0,1:T(8,128)(2,1)} %bitcast.157), channel_id=1, source_target_pairs={{0,2},{1,3},{2,0},{3,1},{4,6},{5,7},{6,4},{7,5},{8,10},{9,11},{10,... | collective-permute-start | bytes 6152 | tf_op jit(solution)/shard_map/ppermute | solution.py:18
  77.1 0.8 slice.136
  78.1 0.7 mul.135
  80.1 0.8 copy.132
  81.5 2.7 %convolution_add_fusion.3 = f32[4,6,64,128]{3,2,1,0:T(8,128)} fusion(f32[4,6,64,128]{3,2,1,0:T(8,128)} %fusion.326, bf16[4,6,128,128]{3,2,1,0:T(8,128)(2,1)S(1)} %bitcast.657, bf16[64,1,6,128]{3,0,2,1:T(8,128)(2,1)} %collective-permute-done, bf16[64,4,6,128]{3,0,2,1:T(8,128)(2,1)S(1)} %copy.110), kind=kOutput, calls=%fused_computation.528 | convolution fusion | flops 51511296 | bytes 2850816 | tf_op jit(solution)/shard_map/rkij,nrkj->nrki/dot_general | solution.py:35
  84.2 0.9 fusion.55
  85.8 1.5 fusion.42
  87.3 1.3 reshape.321
  88.7 0.8 bitcast_bitcast_fusion.1
  89.5 5.2 %collective-permute-start.4 = (bf16[64,128,16]{0,2,1:T(8,128)(2,1)}, bf16[64,128,16]{0,2,1:T(8,128)(2,1)}, u32[]{:S(2)}, u32[]{:S(2)}) collective-permute-start(bf16[64,128,16]{0,2,1:T(8,128)(2,1)} %bitcast_bitcast_fusion.1), channel_id=1, source_target_pairs={{0,2},{1,3},{2,0},{3,1},{4,6},{5,7},{6,4},{7,5},{8,10},{9,11},{10,... | collective-permute-start | bytes 786440 | tf_op jit(solution)/shard_map/ppermute | solution.py:18
  94.7 2.9 %fusion.5 = f32[64,4,6,128]{3,0,2,1:T(8,128)} fusion(f32[4,6,64,128]{3,2,1,0:T(8,128)} %fusion.42, f32[4,6,64,128]{3,2,1,0:T(8,128)} %convolution_add_fusion.3, f32[64,4,5,128]{3,0,2,1:T(8,128)S(1)} %slice-done, f32[64,4,1,128]{3,0,2,1:T(8,128)} %select_bitcast_fusion.5, bf16[64,4,6,128]{3,0,2,1:T(8,128)(2,1)S(1)} %copy.110, ...), kind=kOutput, calls=%fused_computation.527 | convolution fusion | flops 53673984 | bytes 4423680 | tf_op jit(solution)/shard_map/rkji,nrkj->nrki/dot_general | solution.py:39
  97.6 1.6 copy.166
  99.2 20.5 %collective-permute-done.4 = bf16[64,128,16]{0,2,1:T(8,128)(2,1)} collective-permute-done((bf16[64,128,16]{0,2,1:T(8,128)(2,1)}, bf16[64,128,16]{0,2,1:T(8,128)(2,1)}, u32[]{:S(2)}, u32[]{:S(2)}) %collective-permute-start.4) | collective-permute-done | bytes 262176 | tf_op jit(solution)/shard_map/ppermute | solution.py:18
  119.7 7.1 %scatter_custom_fusion = f32[64,3072]{0,1:T(8,128)S(1)} fusion(f32[64,3072]{0,1:T(8,128)S(1)} %bitcast.650, s32[1024]{0:T(1024)} %bitcast.666, bf16[64,128,16]{0,2,1:T(8,128)(2,1)} %collective-permute-done.4, f32[1024]{0:T(1024)S(1)} %mul.125), kind=kCustom, calls=%fused_computation.816 | custom fusion | flops 196608 | bytes 1052672 | tf_op jit(solution)/shard_map/scatter-add | solution.py:118
  126.8 7.5 %scatter_custom_fusion.1 = f32[64,3072]{0,1:T(8,128)S(1)} fusion(f32[64,3072]{0,1:T(8,128)S(1)} %scatter_custom_fusion, s32[1024]{0:T(1024)} %bitcast.668, bf16[64,128,16]{0,2,1:T(8,128)(2,1)} %collective-permute-done.4, f32[1024]{0:T(1024)} %reshape.233), kind=kCustom, calls=%fused_computation.813 | custom fusion | flops 196608 | bytes 1052672 | tf_op jit(solution)/shard_map/scatter-add | solution.py:123
  134.3 1.3 copy.133
  135.6 2.6 %pad_maximum_fusion.1 = (f32[4,16,3072]{2,1,0:T(8,128)}, f32[4,16,3072]{2,1,0:T(8,128)}) fusion(f32[2,16,3072]{2,1,0:T(8,128)} %get-tuple-element.15, f32[2,16,3072]{2,1,0:T(8,128)} %get-tuple-element.14, f32[3072]{0:T(1024)S(1)} %copy-done.15, f32[4,16,3072]{2,1,0:T(8,128)} %bitcast.661, f32[4]{0:T(128)} %constant.42.clone), kind=kLoop, calls=%fused_computation.530 | loop fusion | flops 786432 | bytes 3158032 | tf_op jit(solution)/shard_map/jit(_roll_static)/concatenate | solution.py:128
  138.3 2.8 %copy.149 = f32[64,3072]{0,1:T(8,128)} copy(f32[64,3072]{1,0:T(8,128)} %bitcast.659) | data formatting | bytes 1572864 | tf_op jit(solution)/shard_map/jit(_roll_static)/concatenate | solution.py:128
  141.0 2.8 %add_convert_fusion = bf16[64,3072]{0,1:T(8,128)(2,1)} fusion(f32[64,3072]{0,1:T(8,128)} %copy.149, f32[64,3072]{0,1:T(8,128)S(1)} %scatter_custom_fusion.1, f32[3072]{0:T(1024)S(1)} %copy-done.15, f32[64]{0:T(128)} %mul.136), kind=kLoop, calls=%fused_computation.516 | loop fusion | flops 786432 | bytes 1978624 | tf_op jit(solution)/shard_map/convert_element_type | solution.py:129
  143.8 5.7 %gather_fusion.2 = bf16[1024,64]{1,0:T(8,128)(2,1)} fusion(bf16[64,3072]{0,1:T(8,128)(2,1)} %add_convert_fusion, s32[1024]{0:T(1024)} %copy-done.18), kind=kCustom, calls=%fused_computation.2.clone | custom fusion | bytes 266240 | tf_op jit(solution)/shard_map/jit(_take)/gather | solution.py:100
  149.5 5.6 %gather_fusion.3 = bf16[1024,64]{1,0:T(8,128)(2,1)} fusion(bf16[64,3072]{0,1:T(8,128)(2,1)} %add_convert_fusion, s32[1024]{0:T(1024)} %copy-done.17), kind=kCustom, calls=%fused_computation.3.clone | custom fusion | bytes 266240 | tf_op jit(solution)/shard_map/jit(_take)/gather | solution.py:103
  155.1 2.5 concatenate.53
  157.6 1.3 copy.135
  159.0 2.0 fusion.14
  161.7 1.2 convolution_bitcast_fusion.1
  165.2 0.8 copy-done.13
  166.0 2.1 reshape.322
  168.1 14.0 %all-to-all-start.2 = ((bf16[128,2,512]{2,1,0:T(2,128)(2,1)}), bf16[128,2,512]{2,1,0:T(2,128)(2,1)}, u32[]{:S(2)}, u32[]{:S(2)}) async-start(bf16[128,2,512]{2,1,0:T(2,128)(2,1)} %reshape.322), calls=%async_computation.2 | async-start | bytes 524288 | tf_op jit(solution)/shard_map/all_to_all | solution.py:108
  182.1 2.3 collective-permute-start.6
  184.3 0.9 fusion.53
  185.3 1.9 collective-permute-start.8
  187.2 5.6 %collective-permute-start.7 = (bf16[64,1,6,128]{3,0,1,2:T(8,128)(2,1)}, bf16[64,1,6,128]{3,0,1,2:T(8,128)(2,1)}, u32[]{:S(2)}, u32[]{:S(2)}) collective-permute-start(bf16[64,1,6,128]{3,0,1,2:T(8,128)(2,1)} %get-tuple-element.12), channel_id=1, source_target_pairs={{0,4},{4,8},{8,12},{12,16},{16,20},{20,24},{24,28},{28,32},{32,36}... | collective-permute-start | bytes 294920 | tf_op jit(solution)/shard_map/ppermute | solution.py:26
  192.8 0.8 fusion.322
  194.8 1.5 convolution_add_fusion.1
  197.0 1.5 fusion.15
  198.5 2.2 reshape.323
  200.7 1.9 bitcast_bitcast_fusion
  202.6 4.9 %collective-permute-start.9 = (bf16[64,128,16]{0,2,1:T(8,128)(2,1)}, bf16[64,128,16]{0,2,1:T(8,128)(2,1)}, u32[]{:S(2)}, u32[]{:S(2)}) collective-permute-start(bf16[64,128,16]{0,2,1:T(8,128)(2,1)} %bitcast_bitcast_fusion), channel_id=1, source_target_pairs={{0,2},{1,3},{2,0},{3,1},{4,6},{5,7},{6,4},{7,5},{8,10},{9,11},{10,... | collective-permute-start | bytes 786440 | tf_op jit(solution)/shard_map/ppermute | solution.py:18
  207.5 2.9 %fusion.2 = f32[64,4,6,128]{3,0,1,2:T(8,128)} fusion(f32[4,6,64,128]{3,2,0,1:T(8,128)} %fusion.15, f32[4,6,64,128]{3,2,0,1:T(8,128)} %convolution_add_fusion.1, f32[64,4,5,128]{3,0,1,2:T(8,128)S(1)} %slice-done.1, f32[64,4,1,128]{3,0,1,2:T(8,128)S(1)} %copy-done.14, bf16[64,4,6,128]{3,0,1,2:T(8,128)(2,1)S(1)} %fusion.14, ...), kind=kOutput, calls=%fused_computation.522 | convolution fusion | flops 52494336 | bytes 4423680 | tf_op jit(solution)/shard_map/rkji,nrkj->nrki/dot_general | solution.py:39
  210.4 2.8 %copy.169 = f32[64,4,6,128]{0,3,2,1:T(8,128)} copy(f32[64,4,6,128]{3,0,1,2:T(8,128)} %fusion.2) | data formatting | bytes 1572864 | tf_op jit(solution)/shard_map/reshape | solution.py:98
  213.2 19.7 %collective-permute-done.9 = bf16[64,128,16]{0,2,1:T(8,128)(2,1)} collective-permute-done((bf16[64,128,16]{0,2,1:T(8,128)(2,1)}, bf16[64,128,16]{0,2,1:T(8,128)(2,1)}, u32[]{:S(2)}, u32[]{:S(2)}) %collective-permute-start.9) | collective-permute-done | bytes 262176 | tf_op jit(solution)/shard_map/ppermute | solution.py:18
  232.9 9.4 %scatter_custom_fusion.2 = f32[64,3072]{0,1:T(8,128)} fusion(f32[64,3072]{0,1:T(8,128)} %bitcast.660, s32[1024]{0:T(1024)} %bitcast.667, bf16[64,128,16]{0,2,1:T(8,128)(2,1)} %collective-permute-done.9, f32[1024]{0:T(1024)S(1)} %mul.125), kind=kCustom, calls=%fused_computation.810 | custom fusion | flops 196608 | bytes 1052672 | tf_op jit(solution)/shard_map/scatter-add | solution.py:118
  242.3 9.4 %scatter_custom_fusion.3 = f32[64,3072]{0,1:T(8,128)} fusion(f32[64,3072]{0,1:T(8,128)} %scatter_custom_fusion.2, s32[1024]{0:T(1024)} %bitcast.669, bf16[64,128,16]{0,2,1:T(8,128)(2,1)} %collective-permute-done.9, f32[1024]{0:T(1024)S(1)} %copy-done.16), kind=kCustom, calls=%fused_computation.807 | custom fusion | flops 196608 | bytes 1052672 | tf_op jit(solution)/shard_map/scatter-add | solution.py:123
  251.8 1.9 copy.151
  253.7 1.2 multiply_reduce_fusion.2
  255.0 0.7 pad_maximum_fusion.2
  (364 shorter events, 15.0 us)
Async XLA Ops:
  0.6 49.3 %copy-start = (bf16[24,128,128]{2,1,0:T(8,128)(2,1)S(1)}, bf16[24,128,128]{2,1,0:T(8,128)(2,1)}, u32[]{:S(2)}) copy-start(bf16[24,128,128]{2,1,0:T(8,128)(2,1)} %param.14) | copy-start | bytes 2359300
  0.6 1.8 copy-start.27
  0.7 1.8 copy-start.8
  2.6 15.3 %copy-start.9 = (bf16[24,128,128]{2,1,0:T(8,128)(2,1)S(1)}, bf16[24,128,128]{2,1,0:T(8,128)(2,1)}, u32[]{:S(2)}) copy-start(bf16[24,128,128]{2,1,0:T(8,128)(2,1)} %param.15) | copy-start | bytes 2359300
  3.0 14.9 %copy-start.6 = (f32[64,4,6,128]{3,0,2,1:T(8,128)}, f32[64,4,6,128]{3,0,2,1:T(8,128)S(1)}, u32[]{:S(2)}) copy-start(f32[64,4,6,128]{3,0,2,1:T(8,128)S(1)} %convolution_bitcast_fusion) | copy-start | bytes 2359300
  3.0 18.6 %copy-start.25 = (bf16[128,8]{0,1:T(8,128)(2,1)S(1)}, bf16[128,8]{0,1:T(8,128)(2,1)}, u32[]{:S(2)}) copy-start(bf16[128,8]{0,1:T(8,128)(2,1)} %param.21) | copy-start | bytes 6148
  3.0 18.6 %copy-start.26 = (s32[128]{0:T(128)S(1)}, s32[128]{0:T(128)}, u32[]{:S(2)}) copy-start(s32[128]{0:T(128)} %param.22) | copy-start | bytes 1540
  3.0 32.4 %copy-start.23 = (s32[128,8]{0,1:T(8,128)S(1)}, s32[128,8]{0,1:T(8,128)}, u32[]{:S(2)}) copy-start(s32[128,8]{0,1:T(8,128)} %param.19) | copy-start | bytes 12292
  3.0 32.6 %copy-start.24 = (s32[128,8]{0,1:T(8,128)S(1)}, s32[128,8]{0,1:T(8,128)}, u32[]{:S(2)}) copy-start(s32[128,8]{0,1:T(8,128)} %param.20) | copy-start | bytes 12292
  3.0 34.1 %copy-start.1 = (bf16[4,16,3072]{2,1,0:T(8,128)(2,1)S(1)}, bf16[4,16,3072]{2,1,0:T(8,128)(2,1)}, u32[]{:S(2)}) copy-start(bf16[4,16,3072]{2,1,0:T(8,128)(2,1)} %param.13) | copy-start | bytes 1179652
  3.7 80.5 %collective-permute-start.3 = (f32[64,4,128]{2,0,1:T(8,128)}, f32[64,4,128]{2,0,1:T(8,128)}, u32[]{:S(2)}, u32[]{:S(2)}) collective-permute-start(f32[64,4,128]{2,0,1:T(8,128)} %fusion.54), channel_id=1, source_target_pairs={{0,1},{1,0},{2,3},{3,2},{4,5},{5,4},{6,7},{7,6},{8,9},{9,8},{10,11... | collective-permute-start | bytes 393224 | tf_op jit(solution)/shard_map/ppermute | solution.py:18
  10.2 71.3 %collective-permute-start = (bf16[64,1,6,128]{3,0,2,1:T(8,128)(2,1)}, bf16[64,1,6,128]{3,0,2,1:T(8,128)(2,1)}, u32[]{:S(2)}, u32[]{:S(2)}) collective-permute-start(bf16[64,1,6,128]{3,0,2,1:T(8,128)(2,1)} %get-tuple-element.17), channel_id=1, source_target_pairs={{4,0},{8,4},{12,8},{16,12},{20,16},{24,20},{28,24},{32,28},{36,32}... | collective-permute-start | bytes 294920 | tf_op jit(solution)/shard_map/ppermute | solution.py:29
  13.1 81.7 %collective-permute-start.1 = (bf16[64,1,6,128]{3,0,2,1:T(8,128)(2,1)}, bf16[64,1,6,128]{3,0,2,1:T(8,128)(2,1)}, u32[]{:S(2)}, u32[]{:S(2)}) collective-permute-start(bf16[64,1,6,128]{3,0,2,1:T(8,128)(2,1)} %get-tuple-element.16), channel_id=1, source_target_pairs={{0,4},{4,8},{8,12},{12,16},{16,20},{20,24},{24,28},{28,32},{32,36}... | collective-permute-start | bytes 294920 | tf_op jit(solution)/shard_map/ppermute | solution.py:26
  18.0 0.9 copy-start.2
  19.6 75.1 %collective-permute-start.2 = (bf16[6,128,128]{2,1,0:T(8,128)(2,1)}, bf16[6,128,128]{2,1,0:T(8,128)(2,1)}, u32[]{:S(2)}, u32[]{:S(2)}) collective-permute-start(bf16[6,128,128]{2,1,0:T(8,128)(2,1)} %slice.135), channel_id=1, source_target_pairs={{0,4},{4,8},{8,12},{12,16},{16,20},{20,24},{24,28},{28,32},{32,36}... | collective-permute-start | bytes 589832 | tf_op jit(solution)/shard_map/ppermute | solution.py:14
  22.3 32.6 %all-to-all-start.1 = ((bf16[128,1,8]{2,1,0:T(2,128)(2,1)}), bf16[128,1,8]{2,1,0:T(2,128)(2,1)S(1)}, u32[]{:S(2)}, u32[]{:S(2)}) async-start(bf16[128,1,8]{2,1,0:T(2,128)(2,1)} %copy.130), calls=%async_computation.1 | async-start | bytes 131072 | tf_op jit(solution)/shard_map/all_to_all | solution.py:73
  36.4 5.2 %copy-start.17 = (s32[1024]{0:T(1024)}, s32[1024]{0:T(1024)S(1)}, u32[]{:S(2)}) copy-start(s32[1024]{0:T(1024)S(1)} %get-tuple-element.23) | copy-start | bytes 12292
  36.4 5.2 %copy-start.18 = (s32[1024]{0:T(1024)}, s32[1024]{0:T(1024)S(1)}, u32[]{:S(2)}) copy-start(s32[1024]{0:T(1024)S(1)} %get-tuple-element.22) | copy-start | bytes 12292
  41.6 5.2 %copy-start.20 = (pred[1024]{0:T(1024)(128)(4,1)S(1)}, pred[1024]{0:T(1024)(128)(4,1)}, u32[]{:S(2)}) copy-start(pred[1024]{0:T(1024)(128)(4,1)} %compare_and_fusion.1) | copy-start | bytes 3076
  52.0 0.8 copy-start.12
  52.8 24.2 %copy-start.3 = (bf16[24,128,128]{2,1,0:T(8,128)(2,1)S(1)}, bf16[24,128,128]{2,1,0:T(8,128)(2,1)}, u32[]{:S(2)}) copy-start(bf16[24,128,128]{2,1,0:T(8,128)(2,1)} %copy-done.2) | copy-start | bytes 2359300
  55.0 32.4 %all-to-all-start = ((bf16[128,2,512]{2,1,0:T(2,128)(2,1)}), bf16[128,2,512]{2,1,0:T(2,128)(2,1)}, u32[]{:S(2)}, u32[]{:S(2)}) async-start(bf16[128,2,512]{2,1,0:T(2,128)(2,1)} %reshape.320), calls=%async_computation | async-start | bytes 524288 | tf_op jit(solution)/shard_map/all_to_all | solution.py:108
  68.5 11.6 %collective-permute-start.5 = (bf16[128,8]{0,1:T(8,128)(2,1)}, bf16[128,8]{0,1:T(8,128)(2,1)}, u32[]{:S(2)}, u32[]{:S(2)}) collective-permute-start(bf16[128,8]{0,1:T(8,128)(2,1)} %bitcast.157), channel_id=1, source_target_pairs={{0,2},{1,3},{2,0},{3,1},{4,6},{5,7},{6,4},{7,5},{8,10},{9,11},{10,... | collective-permute-start | bytes 6152 | tf_op jit(solution)/shard_map/ppermute | solution.py:18
  77.0 2.4 copy-start.15
  85.8 8.9 %slice-start = ((f32[64,4,6,128]{3,0,2,1:T(8,128)}), f32[64,4,5,128]{3,0,2,1:T(8,128)S(1)}, s32[]{:S(2)}) async-start(f32[64,4,6,128]{3,0,2,1:T(8,128)} %copy-done.6), calls=%async_computation.3 | async-start | bytes 1310720 | tf_op jit(solution)/shard_map/slice | solution.py:96
  89.5 30.2 %collective-permute-start.4 = (bf16[64,128,16]{0,2,1:T(8,128)(2,1)}, bf16[64,128,16]{0,2,1:T(8,128)(2,1)}, u32[]{:S(2)}, u32[]{:S(2)}) collective-permute-start(bf16[64,128,16]{0,2,1:T(8,128)(2,1)} %bitcast_bitcast_fusion.1), channel_id=1, source_target_pairs={{0,2},{1,3},{2,0},{3,1},{4,6},{5,7},{6,4},{7,5},{8,10},{9,11},{10,... | collective-permute-start | bytes 786440 | tf_op jit(solution)/shard_map/ppermute | solution.py:18
  160.9 1.9 copy-start.11
  160.9 1.9 copy-start.21
  160.9 2.1 copy-start.10
  161.0 2.1 copy-start.19
  165.2 27.7 %copy-start.5 = (f32[4,16,3072]{2,1,0:T(8,128)S(1)}, f32[4,16,3072]{2,1,0:T(8,128)}, u32[]{:S(2)}) copy-start(f32[4,16,3072]{2,1,0:T(8,128)} %get-tuple-element.9) | copy-start | bytes 2359300
  165.2 0.8 copy-start.13
  168.1 30.4 %all-to-all-start.2 = ((bf16[128,2,512]{2,1,0:T(2,128)(2,1)}), bf16[128,2,512]{2,1,0:T(2,128)(2,1)}, u32[]{:S(2)}, u32[]{:S(2)}) async-start(bf16[128,2,512]{2,1,0:T(2,128)(2,1)} %reshape.322), calls=%async_computation.2 | async-start | bytes 524288 | tf_op jit(solution)/shard_map/all_to_all | solution.py:108
  182.1 12.2 %collective-permute-start.6 = (bf16[64,1,6,128]{3,0,1,2:T(8,128)(2,1)}, bf16[64,1,6,128]{3,0,1,2:T(8,128)(2,1)S(1)}, u32[]{:S(2)}, u32[]{:S(2)}) collective-permute-start(bf16[64,1,6,128]{3,0,1,2:T(8,128)(2,1)} %get-tuple-element.13), channel_id=1, source_target_pairs={{4,0},{8,4},{12,8},{16,12},{20,16},{24,20},{28,24},{32,28},{36,32}... | collective-permute-start | bytes 294920 | tf_op jit(solution)/shard_map/ppermute | solution.py:29
  185.3 11.0 %collective-permute-start.8 = (f32[64,4,128]{2,0,1:T(8,128)S(1)}, f32[64,4,128]{2,0,1:T(8,128)S(1)}, u32[]{:S(2)}, u32[]{:S(2)}) collective-permute-start(f32[64,4,128]{2,0,1:T(8,128)S(1)} %fusion.53), channel_id=1, source_target_pairs={{0,1},{1,0},{2,3},{3,2},{4,5},{5,4},{6,7},{7,6},{8,9},{9,8},{10,11... | collective-permute-start | bytes 393224 | tf_op jit(solution)/shard_map/ppermute | solution.py:18
  187.2 20.3 %collective-permute-start.7 = (bf16[64,1,6,128]{3,0,1,2:T(8,128)(2,1)}, bf16[64,1,6,128]{3,0,1,2:T(8,128)(2,1)}, u32[]{:S(2)}, u32[]{:S(2)}) collective-permute-start(bf16[64,1,6,128]{3,0,1,2:T(8,128)(2,1)} %get-tuple-element.12), channel_id=1, source_target_pairs={{0,4},{4,8},{8,12},{12,16},{16,20},{20,24},{24,28},{28,32},{32,36}... | collective-permute-start | bytes 294920 | tf_op jit(solution)/shard_map/ppermute | solution.py:26
  193.6 1.1 copy-start.4
  198.5 9.0 %slice-start.1 = ((f32[64,4,6,128]{3,0,1,2:T(8,128)}), f32[64,4,5,128]{3,0,1,2:T(8,128)S(1)}, s32[]{:S(2)}) async-start(f32[64,4,6,128]{3,0,1,2:T(8,128)} %convolution_bitcast_fusion.1), calls=%async_computation.4 | async-start | bytes 1310720 | tf_op jit(solution)/shard_map/slice | solution.py:96
  198.5 9.0 %copy-start.14 = (f32[64,4,1,128]{3,0,1,2:T(8,128)S(1)}, f32[64,4,1,128]{3,0,1,2:T(8,128)}, u32[]{:S(2)}) copy-start(f32[64,4,1,128]{3,0,1,2:T(8,128)} %select_bitcast_fusion.4) | copy-start | bytes 393220
  202.6 30.3 %collective-permute-start.9 = (bf16[64,128,16]{0,2,1:T(8,128)(2,1)}, bf16[64,128,16]{0,2,1:T(8,128)(2,1)}, u32[]{:S(2)}, u32[]{:S(2)}) collective-permute-start(bf16[64,128,16]{0,2,1:T(8,128)(2,1)} %bitcast_bitcast_fusion), channel_id=1, source_target_pairs={{0,2},{1,3},{2,0},{3,1},{4,6},{5,7},{6,4},{7,5},{8,10},{9,11},{10,... | collective-permute-start | bytes 786440 | tf_op jit(solution)/shard_map/ppermute | solution.py:18
  210.4 31.9 %copy-start.16 = (f32[1024]{0:T(1024)S(1)}, f32[1024]{0:T(1024)}, u32[]{:S(2)}) copy-start(f32[1024]{0:T(1024)} %reshape.233) | copy-start | bytes 12292
  251.8 1.9 copy-start.7
  251.8 1.9 copy-start.22
